TPU v7x, 256 devices: a whole 4x4x8 slice. The times are simulated.
256 devices in a mesh: section: 16 (over x, y_lo, core), dp: 8 (over z), tensor: 2 (over y_hi).
Axes of the slice: x: 4, y: 4 (y_hi: 2, y_lo: 2; y = y_hi * 2 + y_lo), z: 8, core: 2. Of those that a mesh axis runs over, the one named last changes fastest.
Arguments:
- activations: bfloat16 [16, 8192, 2048], P('section', 'dp', 'tensor'), may hold values from -150 to 150, as said below
- sent_grads: bfloat16 [16, 8192, 2048], P('section', 'dp', 'tensor'), may hold values from -150 to 150, as said below
- damping: float32 [16, 2, 2], P('section', None, 'tensor'), may hold values from 0.05 to 0.5
- bubble_steps: int32 [16, 2, 2], P('section', None, 'tensor'), may hold values from 1 to 3
- warm: float32 [16, 2, 2, 1024, 1024], P('section', None, 'tensor', 'dp'), may hold values from -0.02 to 1.2, as said below
Outputs:
- inverse: float32 [16, 2, 2, 1024, 1024], P('section', None, 'tensor', 'dp')
Inputs may be any that keep to these rules, and one draw needn't show every extreme that they name: `activations`: input features of one section's layer, rows and columns of differing scales. `sent_grads`: gradients of one section's layer outputs, rows and columns of differing scales. `warm`: symmetric with a positive diagonal; Newton-Schulz steps from it contract toward the inverse of each block's factor.
All inputs are finite; a program needn't handle non-finite values.
Results may differ from a plain program's by a relative error of at most 0.0003.
Values may be sent and summed in bfloat16 or wider, within the bound.
A program may use at most 192 MiB of HBM per device.

v0:
```python
import jax
import jax.numpy as jnp
from jax import lax
from jax.sharding import PartitionSpec as P

ITERS = 3


def from_behind(value, axis, steps):
    count = lax.axis_size(axis)
    leading, last = (max(0, -steps), min(count, count - steps))
    return lax.ppermute(value, axis, [(source, source + steps) for source in range(leading, last)])


def gram(rows):
    return lax.dot_general(rows, rows, (((0,), (0,)), ((), ())), preferred_element_type=jnp.float32)


def fetch_grads(sent_grads):
    return from_behind(sent_grads, "section", -1)


def newton_step(iterates, factors, counts, index):
    products = tuple(
        (jnp.dot(x, f, precision=lax.Precision.HIGHEST) for x, f in zip(iterates, factors))
    )
    pieces = jax.tree.map(lambda part: lax.all_gather(part, "dp", axis=0, tiled=True), iterates)
    folded = tuple(
        (
            jnp.dot(product, piece, precision=lax.Precision.HIGHEST)
            for product, piece in zip(products, pieces)
        )
    )
    return tuple(
        (jnp.where(index < count, 2.0 * x - t, x) for x, t, count in zip(iterates, folded, counts))
    )


def local(activations, sent_grads, damping, bubble_steps, warm):
    inputs = activations[0]
    received = fetch_grads(sent_grads)
    first_part = gram(inputs)
    second_part = gram(received[0])
    first_sum, second_sum = lax.psum((first_part, second_part), "dp")
    total_tokens = inputs.shape[0] * lax.axis_size("dp")
    identity = jnp.eye(first_sum.shape[0], dtype=jnp.float32)
    factors = (
        first_sum / total_tokens + damping[0, 0, 0] * identity,
        second_sum / total_tokens + damping[0, 1, 0] * identity,
    )
    counts = (bubble_steps[0, 0, 0], bubble_steps[0, 1, 0])
    iterates = (warm[0, 0, 0], warm[0, 1, 0])
    for index in range(ITERS):
        iterates = newton_step(iterates, factors, counts, index)
    return jnp.stack(iterates)[None, :, None]


def solution(mesh):
    placed = (
        P("section", "dp", "tensor"),
        P("section", "dp", "tensor"),
        P("section", None, "tensor"),
        P("section", None, "tensor"),
        P("section", None, "tensor", "dp", None),
    )
    return jax.shard_map(
        local,
        mesh=mesh,
        in_specs=placed,
        out_specs=P("section", None, "tensor", "dp", None),
        check_vma=False,
    )
```

profile of v0, /device:TPU:1, one launch (start us, length us, event | category | flops | bytes accessed | tf_op | source)
XLA Modules:
  0.0 574.6 jit_solution(16592266944513606604)
XLA Ops:
  6.5 5.2 collective-permute-start
  11.8 4.4 fusion.12
  16.2 19.0 %collective-permute-done = bf16[1,1024,1024]{2,1,0:T(8,128)(2,1)S(1)} collective-permute-done((bf16[1,1024,1024]{2,1,0:T(8,128)(2,1)}, bf16[1,1024,1024]{2,1,0:T(8,128)(2,1)S(1)}, u32[]{:S(2)}, u32[]{:S(2)}) %collective-permute-start) | collective-permute-done | bytes 2097184 | tf_op jit(solution)/shard_map/ppermute | solution.py:12
  35.2 4.4 fusion.10
  39.6 1.1 copy-done.5
  40.8 1.1 fusion.66
  41.9 0.7 all-gather.19.cloned.1.call-update
  42.6 0.6 all-gather.9.cloned.1.call-start
  43.2 0.6 fusion.67
  44.3 0.6 fusion.68
  44.9 185.7 %all-reduce.3.cloned.1.call-done = (f32[1024,1024]{1,0:T(8,128)}, f32[1024,1024]{1,0:T(8,128)}) async-done(((f32[1024,1024]{1,0:T(8,128)}, f32[1024,1024]{1,0:T(8,128)}), (f32[1024,1024]{1,0:T(8,128)}, f32[1024,1024]{1,0:T(8,128)})) %all-reduce.3.cloned.1.call-update) | async-done | bytes 8388624 | tf_op jit(solution)/shard_map/psum | solution.py:44
  230.6 10.3 %fusion.6 = f32[1024,128]{1,0:T(8,128)} fusion(f32[1024,1024]{1,0:T(8,128)} %get-tuple-element.6, f32[]{:T(128)} %bitcast.5, f32[1,2,1,128,1024]{4,3,2,1,0:T(8,128)S(1)} %copy-done.5), kind=kOutput, calls=%fused_computation.9 | convolution fusion | flops 1614807040 | bytes 5242884 | tf_op jit(solution)/shard_map/dot_general | solution.py:25
  240.9 45.1 %all-gather.17.cloned.1.call-done = f32[1,1,1,1024,1024]{4,3,2,1,0:T(8,128)} async-done(((f32[1,1,1,128,1024]{4,3,2,1,0:T(8,128)}), f32[1,1,1,1024,1024]{4,3,2,1,0:T(8,128)}) %all-gather.17.cloned.1.call-update) | async-done | bytes 4194320 | tf_op jit(solution)/shard_map/all_gather | solution.py:27
  285.9 5.5 fusion.35
  291.5 0.2 all-gather.13.cloned.1.call-start
  292.3 10.3 %fusion.9 = f32[1024,128]{1,0:T(8,128)} fusion(f32[1024,1024]{1,0:T(8,128)} %get-tuple-element.5, f32[]{:T(128)} %bitcast.13, f32[1,2,1,128,1024]{4,3,2,1,0:T(8,128)S(1)} %copy-done.5), kind=kOutput, calls=%fused_computation.12 | convolution fusion | flops 1614807040 | bytes 5242884 | tf_op jit(solution)/shard_map/dot_general | solution.py:25
  302.6 38.5 %all-gather.19.cloned.1.call-done = f32[1,1,1,1024,1024]{4,3,2,1,0:T(8,128)} async-done(((f32[1,1,1,128,1024]{4,3,2,1,0:T(8,128)}), f32[1,1,1,1024,1024]{4,3,2,1,0:T(8,128)}) %all-gather.19.cloned.1.call-update) | async-done | bytes 4194320 | tf_op jit(solution)/shard_map/all_gather | solution.py:27
  341.1 5.6 fusion.41
  347.4 6.2 %fusion.5 = f32[128,1024]{1,0:T(8,128)} fusion(f32[128,1024]{1,0:T(8,128)S(1)} %copy-done.2, f32[1024,1024]{1,0:T(8,128)} %get-tuple-element.6, f32[]{:T(128)} %bitcast.5), kind=kOutput, calls=%fused_computation.8 | convolution fusion | flops 1614807040 | bytes 5242884 | tf_op jit(solution)/shard_map/dot_general | solution.py:25
  353.6 42.6 %all-gather.9.cloned.1.call-done = f32[1024,1024]{1,0:T(8,128)} async-done(((f32[128,1024]{1,0:T(8,128)}), f32[1024,1024]{1,0:T(8,128)}) %all-gather.9.cloned.1.call-update) | async-done | bytes 4194320 | tf_op jit(solution)/shard_map/all_gather | solution.py:27
  396.2 5.6 fusion.49
  401.8 0.3 all-gather.15.cloned.1.call-start
  402.6 6.2 %fusion.8 = f32[128,1024]{1,0:T(8,128)} fusion(f32[128,1024]{1,0:T(8,128)S(1)} %copy-done.3, f32[1024,1024]{1,0:T(8,128)} %get-tuple-element.5, f32[]{:T(128)} %bitcast.13), kind=kOutput, calls=%fused_computation.11 | convolution fusion | flops 1614807040 | bytes 5242884 | tf_op jit(solution)/shard_map/dot_general | solution.py:25
  408.8 42.4 %all-gather.13.cloned.1.call-done = f32[1024,1024]{1,0:T(8,128)} async-done(((f32[128,1024]{1,0:T(8,128)}), f32[1024,1024]{1,0:T(8,128)}) %all-gather.13.cloned.1.call-update) | async-done | bytes 4194320 | tf_op jit(solution)/shard_map/all_gather | solution.py:27
  451.2 5.6 fusion.46
  458.4 6.2 %fusion.4 = f32[128,1024]{1,0:T(8,128)} fusion(f32[128,1024]{1,0:T(8,128)S(1)} %copy-done.1, f32[1024,1024]{1,0:T(8,128)} %get-tuple-element.6, f32[]{:T(128)} %bitcast.5), kind=kOutput, calls=%fused_computation.7 | convolution fusion | flops 1614807040 | bytes 5242884 | tf_op jit(solution)/shard_map/dot_general | solution.py:25
  464.6 4.0 fusion.7
  468.6 37.6 %all-gather.11.cloned.1.call-done = f32[1024,1024]{1,0:T(8,128)} async-done(((f32[128,1024]{1,0:T(8,128)}), f32[1024,1024]{1,0:T(8,128)}) %all-gather.11.cloned.1.call-update) | async-done | bytes 4194320 | tf_op jit(solution)/shard_map/all_gather | solution.py:27
  506.2 5.6 fusion.48
  511.8 49.6 %all-gather.15.cloned.1.call-done = f32[1024,1024]{1,0:T(8,128)} async-done(((f32[128,1024]{1,0:T(8,128)}), f32[1024,1024]{1,0:T(8,128)}) %all-gather.15.cloned.1.call-update) | async-done | bytes 4194320 | tf_op jit(solution)/shard_map/all_gather | solution.py:27
  561.6 4.8 fusion.45
  566.4 1.0 maximum_bitcast_fusion
  (29 shorter events, 0.3 us)
Async XLA Ops:
  6.5 5.2 copy-start
  6.5 224.1 %all-reduce.3.cloned.1.call-start = ((), (), s32[]{:S(2)}) async-start(), calls=%async_computation.6 | async-start | bytes 16777216 | tf_op jit(solution)/shard_map/psum | solution.py:44
  6.5 28.6 %collective-permute-start = (bf16[1,1024,1024]{2,1,0:T(8,128)(2,1)}, bf16[1,1024,1024]{2,1,0:T(8,128)(2,1)S(1)}, u32[]{:S(2)}, u32[]{:S(2)}) collective-permute-start(bf16[1,1024,1024]{2,1,0:T(8,128)(2,1)} %param.6), channel_id=1, source_target_pairs={{16,0},{32,16},{48,32},{64,48},{80,64},{96,80},{112,96},{128,112},... | collective-permute-start | bytes 6291464 | tf_op jit(solution)/shard_map/ppermute | solution.py:12
  39.5 1.2 copy-start.5
  39.5 3.6 copy-start.7
  39.5 4.7 copy-start.8
  39.6 246.4 %all-gather.17.cloned.1.call-start = ((), (), s32[]{:S(2)}) async-start(), calls=%async_computation.4 | async-start | bytes 4718592 | tf_op jit(solution)/shard_map/all_gather | solution.py:27
  41.8 299.3 %all-gather.19.cloned.1.call-start = ((), (), s32[]{:S(2)}) async-start(), calls=%async_computation.5 | async-start | bytes 4718592 | tf_op jit(solution)/shard_map/all_gather | solution.py:27
  42.6 353.6 %all-gather.9.cloned.1.call-start = ((), (), s32[]{:S(2)}) async-start(), calls=%async_computation | async-start | bytes 4718592 | tf_op jit(solution)/shard_map/all_gather | solution.py:27
  291.5 159.7 %all-gather.13.cloned.1.call-start = ((), (), s32[]{:S(2)}) async-start(), calls=%async_computation.2 | async-start | bytes 4718592 | tf_op jit(solution)/shard_map/all_gather | solution.py:27
  302.6 44.8 %copy-start.2 = (f32[128,1024]{1,0:T(8,128)S(1)}, f32[128,1024]{1,0:T(8,128)}, u32[]{:S(2)}) copy-start(f32[128,1024]{1,0:T(8,128)} %fusion.35) | copy-start | bytes 1572868
  346.8 159.4 %all-gather.11.cloned.1.call-start = ((), (), s32[]{:S(2)}) async-start(), calls=%async_computation.1 | async-start | bytes 4718592 | tf_op jit(solution)/shard_map/all_gather | solution.py:27
  353.6 49.0 %copy-start.3 = (f32[128,1024]{1,0:T(8,128)S(1)}, f32[128,1024]{1,0:T(8,128)}, u32[]{:S(2)}) copy-start(f32[128,1024]{1,0:T(8,128)} %fusion.41) | copy-start | bytes 1572868
  401.8 159.6 %all-gather.15.cloned.1.call-start = ((), (), s32[]{:S(2)}) async-start(), calls=%async_computation.3 | async-start | bytes 4718592 | tf_op jit(solution)/shard_map/all_gather | solution.py:27
  408.8 49.6 %copy-start.1 = (f32[128,1024]{1,0:T(8,128)S(1)}, f32[128,1024]{1,0:T(8,128)}, u32[]{:S(2)}) copy-start(f32[128,1024]{1,0:T(8,128)} %fusion.49) | copy-start | bytes 1572868
  456.7 7.9 %copy-start.4 = (f32[128,1024]{1,0:T(8,128)S(1)}, f32[128,1024]{1,0:T(8,128)}, u32[]{:S(2)}) copy-start(f32[128,1024]{1,0:T(8,128)} %fusion.46) | copy-start | bytes 1572868
  456.8 7.8 %copy-start.9 = (f32[1024,1024]{1,0:T(8,128)S(1)}, f32[1024,1024]{1,0:T(8,128)}, u32[]{:S(2)}) copy-start(f32[1024,1024]{1,0:T(8,128)} %get-tuple-element.5) | copy-start | bytes 12582916
  511.8 54.6 %copy-start.6 = (f32[1,128,1024]{2,1,0:T(8,128)S(1)}, f32[1,128,1024]{2,1,0:T(8,128)}, u32[]{:S(2)}) copy-start(f32[1,128,1024]{2,1,0:T(8,128)} %fusion.48) | copy-start | bytes 1572868
Sparse Core Ops, SparseCore 0:
  39.7 190.8 all-reduce.2
  232.4 53.4 all-gather.16
  287.7 53.3 all-gather.18
  342.8 53.3 all-gather.8
  397.8 53.3 all-gather.12
  452.8 53.3 all-gather.10
  508.0 53.3 all-gather.14
where the time goes:
time: 579 us; the launch traced here: 575 us
  waiting for transfers between devices  461 us (80%)
  matrix products  84.6 us (15%)
  between operations  17.9 us (3%)
  starting transfers between devices  6.39 us (1%)
    all_gather x6, waiting for transfers between devices, newton_step(): lax.all_gather(part, 'dp', axis=0, tiled=True)  256 us
    psum x1, waiting for transfers between devices, local(): first_sum, second_sum = lax.psum((first_part, second_part), 'dp')  186 us
    dot_general x6, matrix products, newton_step(): jnp.dot(x, f, precision=lax.Precision.HIGHEST)  43.1 us
    dot_general x6, matrix products, newton_step(): jnp.dot(product, piece, precision=lax.Precision.HIGHEST)  32.7 us
    ppermute x1, waiting for transfers between devices, from_behind(): lax.ppermute(value, axis, [(source, source + steps) for source in range(l...  19 us
  transfers between devices with their start and end apart: 8, of which 8 were waited for; matrix products, arithmetic and copies ran while one was open for 14% of the time, Pallas kernels for 0%

commit v1 on v0

--- a/solution.py
+++ b/solution.py
@@ -4,6 +4,34 @@
 from jax.sharding import PartitionSpec as P
 
 ITERS = 3
+
+
+def _mix_case(my_tile, out_dim):
+    my_tile = jnp.moveaxis(my_tile, 0, out_dim)
+    x_next = my_tile.shape
+    met_up = my_tile.reshape(
+        *x_next[:out_dim], x_next[out_dim] * x_next[out_dim + 1], *x_next[out_dim + 2 :]
+    )
+    return met_up
+
+
+def serve_the_area(dim_at, z_in, shard_axis):
+    width = lax.axis_size(shard_axis)
+    log = [(src_i, (src_i + 1) % width) for src_i in range(width)]
+    items = [(tick, dd) for dd, tick in log]
+    low, later = ([], [])
+    for dev in range(width - 1):
+        if dev % 2 == 0:
+            low.append(lax.ppermute(low[-1] if low else z_in, shard_axis, perm=log))
+        else:
+            later.append(
+                lax.ppermute(later[-1] if later else z_in, axis_name=shard_axis, perm=items)
+            )
+    m_next = jnp.stack([*low[::-1], z_in, *later], 0)
+    big = lax.axis_index(shard_axis) - len(low)
+    m_next = m_next[(jnp.arange(width) - big) % width]
+    next_value = _mix_case(m_next, dim_at)
+    return next_value
 
 
 def from_behind(value, axis, steps):
@@ -24,7 +52,7 @@
     products = tuple(
         (jnp.dot(x, f, precision=lax.Precision.HIGHEST) for x, f in zip(iterates, factors))
     )
-    pieces = jax.tree.map(lambda part: lax.all_gather(part, "dp", axis=0, tiled=True), iterates)
+    pieces = jax.tree.map(lambda part: serve_the_area(0, part, "dp"), iterates)
     folded = tuple(
         (
             jnp.dot(product, piece, precision=lax.Precision.HIGHEST)

time: 579 us -> 569 us (0.983)
  the two profiles are of different devices: /device:TPU:1 before, /device:TPU:2 now
where the time goes in v1:
time: 569 us; the launch traced here: 559 us
  waiting for transfers between devices  336 us (59%)
  local copies, waits for them, and re-layouts  87.8 us (15%)
  matrix products  62.3 us (11%)
  starting transfers between devices  53.7 us (9%)
  between operations  18 us (3%)
    ppermute x24, waiting for transfers between devices, serve_the_area(): low.append(lax.ppermute(low[-1] if low else z_in, shard_axis, perm=log))  247 us
    psum x1, waiting for transfers between devices, local(): first_sum, second_sum = lax.psum((first_part, second_part), 'dp')  68.1 us
    unnamed x77, local copies, waits for them, and re-layouts  47.5 us
    ppermute x18, starting transfers between devices, serve_the_area(): lax.ppermute(later[-1] if later else z_in, axis_name=shard_axis, perm=items)  36.6 us
    dot_general x6, matrix products, newton_step(): jnp.dot(x, f, precision=lax.Precision.HIGHEST)  31.8 us
    gather x6, local copies, waits for them, and re-layouts, serve_the_area(): m_next = m_next[(jnp.arange(width) - big) % width]  30.5 us
    dot_general x6, matrix products, newton_step(): jnp.dot(product, piece, precision=lax.Precision.HIGHEST)  21.7 us
    ppermute x1, waiting for transfers between devices, from_behind(): lax.ppermute(value, axis, [(source, source + steps) for source in range(l...  19.5 us
  transfers between devices with their start and end apart: 44, of which 24 were waited for; matrix products, arithmetic and copies ran while one was open for 21% of the time, Pallas kernels for 0%

profile of v1, /device:TPU:2, one launch (start us, length us, event | category | flops | bytes accessed | tf_op | source)
XLA Modules:
  0.0 559.0 jit_solution(9943215048810233183)
XLA Ops:
  13.9 19.5 %collective-permute-done.21 = bf16[1,1024,1024]{2,1,0:T(8,128)(2,1)S(1)} collective-permute-done((bf16[1,1024,1024]{2,1,0:T(8,128)(2,1)}, bf16[1,1024,1024]{2,1,0:T(8,128)(2,1)S(1)}, u32[]{:S(2)}, u32[]{:S(2)}) %collective-permute-start.21) | collective-permute-done | bytes 2097184 | tf_op jit(solution)/shard_map/ppermute | solution.py:40
  33.4 4.5 fusion.6
  43.1 16.2 %collective-permute-done.22 = f32[128,1024]{1,0:T(8,128)S(1)} collective-permute-done((f32[128,1024]{1,0:T(8,128)S(1)}, f32[128,1024]{1,0:T(8,128)S(1)}, u32[]{:S(2)}, u32[]{:S(2)}) %collective-permute-start.22) | collective-permute-done | bytes 524320 | tf_op jit(solution)/shard_map/ppermute | solution.py:25
  64.2 17.6 %collective-permute-done = f32[128,1024]{1,0:T(8,128)S(1)} collective-permute-done((f32[128,1024]{1,0:T(8,128)S(1)}, f32[128,1024]{1,0:T(8,128)S(1)}, u32[]{:S(2)}, u32[]{:S(2)}) %collective-permute-start) | collective-permute-done | bytes 524320 | tf_op jit(solution)/shard_map/ppermute | solution.py:25
  81.8 22.5 %collective-permute-done.23 = f32[128,1024]{1,0:T(8,128)S(1)} collective-permute-done((f32[128,1024]{1,0:T(8,128)S(1)}, f32[128,1024]{1,0:T(8,128)S(1)}, u32[]{:S(2)}, u32[]{:S(2)}) %collective-permute-start.23) | collective-permute-done | bytes 524320 | tf_op jit(solution)/shard_map/ppermute | solution.py:25
  112.3 14.6 %collective-permute-done.1 = f32[128,1024]{1,0:T(8,128)} collective-permute-done((f32[128,1024]{1,0:T(8,128)S(1)}, f32[128,1024]{1,0:T(8,128)}, u32[]{:S(2)}, u32[]{:S(2)}) %collective-permute-start.1) | collective-permute-done | bytes 524320 | tf_op jit(solution)/shard_map/ppermute | solution.py:25
  127.3 22.0 %collective-permute-done.24 = f32[128,1024]{1,0:T(8,128)} collective-permute-done((f32[128,1024]{1,0:T(8,128)S(1)}, f32[128,1024]{1,0:T(8,128)}, u32[]{:S(2)}, u32[]{:S(2)}) %collective-permute-start.24) | collective-permute-done | bytes 524320 | tf_op jit(solution)/shard_map/ppermute | solution.py:25
  157.2 14.6 %collective-permute-done.2 = f32[128,1024]{1,0:T(8,128)} collective-permute-done((f32[128,1024]{1,0:T(8,128)}, f32[128,1024]{1,0:T(8,128)}, u32[]{:S(2)}, u32[]{:S(2)}) %collective-permute-start.2) | collective-permute-done | bytes 524320 | tf_op jit(solution)/shard_map/ppermute | solution.py:25
  171.8 22.5 %collective-permute-done.25 = f32[128,1024]{1,0:T(8,128)} collective-permute-done((f32[128,1024]{1,0:T(8,128)}, f32[128,1024]{1,0:T(8,128)}, u32[]{:S(2)}, u32[]{:S(2)}) %collective-permute-start.25) | collective-permute-done | bytes 524320 | tf_op jit(solution)/shard_map/ppermute | solution.py:25
  200.8 14.4 %collective-permute-done.3 = f32[128,1024]{1,0:T(8,128)S(1)} collective-permute-done((f32[128,1024]{1,0:T(8,128)}, f32[128,1024]{1,0:T(8,128)S(1)}, u32[]{:S(2)}, u32[]{:S(2)}) %collective-permute-start.3) | collective-permute-done | bytes 524320 | tf_op jit(solution)/shard_map/ppermute | solution.py:25
  225.4 5.4 gather_fusion
  235.5 5.1 gather_fusion.3
  240.6 68.1 %all-reduce.3.cloned.1.call-done = (f32[1024,1024]{1,0:T(8,128)}, f32[1024,1024]{1,0:T(8,128)}) async-done(((f32[1024,1024]{1,0:T(8,128)}, f32[1024,1024]{1,0:T(8,128)}), (f32[1024,1024]{1,0:T(8,128)}, f32[1024,1024]{1,0:T(8,128)})) %all-reduce.3.cloned.1.call-update) | async-done | bytes 8388624 | tf_op jit(solution)/shard_map/psum | solution.py:72
  308.7 9.8 %fusion.2 = f32[1024,128]{1,0:T(8,128)S(1)} fusion(f32[1024,1024]{1,0:T(8,128)} %get-tuple-element.6, f32[]{:T(128)} %bitcast.5, f32[1,2,1,128,1024]{4,3,2,1,0:T(8,128)S(1)} %copy-done.5), kind=kOutput, calls=%fused_computation.11 | convolution fusion | flops 1614807040 | bytes 5242884 | tf_op jit(solution)/shard_map/dot_general | solution.py:53
  321.3 7.5 %fusion.5 = f32[1024,128]{1,0:T(8,128)S(1)} fusion(f32[1024,1024]{1,0:T(8,128)S(1)} %copy-done.14, f32[]{:T(128)} %bitcast.40, f32[1,2,1,128,1024]{4,3,2,1,0:T(8,128)S(1)} %copy-done.5), kind=kOutput, calls=%fused_computation.14 | convolution fusion | flops 1614807040 | bytes 5242884 | tf_op jit(solution)/shard_map/dot_general | solution.py:53
  340.4 8.0 %collective-permute-done.29 = f32[128,1024]{1,0:T(8,128)S(1)} collective-permute-done((f32[128,1024]{1,0:T(8,128)S(1)}, f32[128,1024]{1,0:T(8,128)S(1)}, u32[]{:S(2)}, u32[]{:S(2)}) %collective-permute-start.29) | collective-permute-done | bytes 524320 | tf_op jit(solution)/shard_map/ppermute | solution.py:25
  348.6 11.0 %collective-permute-done.8 = f32[128,1024]{1,0:T(8,128)S(1)} collective-permute-done((f32[128,1024]{1,0:T(8,128)S(1)}, f32[128,1024]{1,0:T(8,128)S(1)}, u32[]{:S(2)}, u32[]{:S(2)}) %collective-permute-start.8) | collective-permute-done | bytes 524320 | tf_op jit(solution)/shard_map/ppermute | solution.py:25
  364.3 6.5 %collective-permute-done.30 = f32[128,1024]{1,0:T(8,128)S(1)} collective-permute-done((f32[128,1024]{1,0:T(8,128)S(1)}, f32[128,1024]{1,0:T(8,128)S(1)}, u32[]{:S(2)}, u32[]{:S(2)}) %collective-permute-start.30) | collective-permute-done | bytes 524320 | tf_op jit(solution)/shard_map/ppermute | solution.py:25
  370.8 11.2 %collective-permute-done.9 = f32[128,1024]{1,0:T(8,128)S(1)} collective-permute-done((f32[128,1024]{1,0:T(8,128)S(1)}, f32[128,1024]{1,0:T(8,128)S(1)}, u32[]{:S(2)}, u32[]{:S(2)}) %collective-permute-start.9) | collective-permute-done | bytes 524320 | tf_op jit(solution)/shard_map/ppermute | solution.py:25
  394.3 10.2 %collective-permute-done.10 = f32[128,1024]{1,0:T(8,128)S(1)} collective-permute-done((f32[128,1024]{1,0:T(8,128)S(1)}, f32[128,1024]{1,0:T(8,128)S(1)}, u32[]{:S(2)}, u32[]{:S(2)}) %collective-permute-start.10) | collective-permute-done | bytes 524320 | tf_op jit(solution)/shard_map/ppermute | solution.py:25
  411.2 5.1 gather_fusion.1
  416.3 4.7 fusion.34
  432.0 4.9 gather_fusion.4
  436.9 4.7 fusion.30
  447.1 10.7 %collective-permute-done.36 = f32[128,1024]{1,0:T(8,128)S(1)} collective-permute-done((f32[128,1024]{1,0:T(8,128)S(1)}, f32[128,1024]{1,0:T(8,128)S(1)}, u32[]{:S(2)}, u32[]{:S(2)}) %collective-permute-start.36) | collective-permute-done | bytes 524320 | tf_op jit(solution)/shard_map/ppermute | solution.py:25
  458.4 10.6 %collective-permute-done.15 = f32[128,1024]{1,0:T(8,128)S(1)} collective-permute-done((f32[128,1024]{1,0:T(8,128)S(1)}, f32[128,1024]{1,0:T(8,128)S(1)}, u32[]{:S(2)}, u32[]{:S(2)}) %collective-permute-start.15) | collective-permute-done | bytes 524320 | tf_op jit(solution)/shard_map/ppermute | solution.py:25
  474.7 5.6 collective-permute-done.37
  480.9 10.6 %collective-permute-done.16 = f32[128,1024]{1,0:T(8,128)S(1)} collective-permute-done((f32[128,1024]{1,0:T(8,128)S(1)}, f32[128,1024]{1,0:T(8,128)S(1)}, u32[]{:S(2)}, u32[]{:S(2)}) %collective-permute-start.16) | collective-permute-done | bytes 524320 | tf_op jit(solution)/shard_map/ppermute | solution.py:25
  505.0 8.9 %collective-permute-done.17 = f32[128,1024]{1,0:T(8,128)S(1)} collective-permute-done((f32[128,1024]{1,0:T(8,128)S(1)}, f32[128,1024]{1,0:T(8,128)S(1)}, u32[]{:S(2)}, u32[]{:S(2)}) %collective-permute-start.17) | collective-permute-done | bytes 524320 | tf_op jit(solution)/shard_map/ppermute | solution.py:25
  528.8 5.0 gather_fusion.2
  538.5 5.0 gather_fusion.5
  543.5 4.9 fusion.33
  (166 shorter events, 149.1 us)
Async XLA Ops:
  6.5 302.2 %all-reduce.3.cloned.1.call-start = ((), (), s32[]{:S(2)}) async-start(), calls=%async_computation | async-start | bytes 16777216 | tf_op jit(solution)/shard_map/psum | solution.py:72
  6.5 26.9 %collective-permute-start.21 = (bf16[1,1024,1024]{2,1,0:T(8,128)(2,1)}, bf16[1,1024,1024]{2,1,0:T(8,128)(2,1)S(1)}, u32[]{:S(2)}, u32[]{:S(2)}) collective-permute-start(bf16[1,1024,1024]{2,1,0:T(8,128)(2,1)} %param.6), channel_id=1, source_target_pairs={{16,0},{32,16},{48,32},{64,48},{80,64},{96,80},{112,96},{128,112},... | collective-permute-start | bytes 6291464 | tf_op jit(solution)/shard_map/ppermute | solution.py:40
  41.2 40.6 %collective-permute-start = (f32[128,1024]{1,0:T(8,128)S(1)}, f32[128,1024]{1,0:T(8,128)S(1)}, u32[]{:S(2)}, u32[]{:S(2)}) collective-permute-start(f32[128,1024]{1,0:T(8,128)S(1)} %get-tuple-element.9), channel_id=1, source_target_pairs={{0,2},{2,4},{4,6},{6,8},{8,10},{10,12},{12,14},{14,0},{1,3},{3,5},... | collective-permute-start | bytes 1572872 | tf_op jit(solution)/shard_map/ppermute | solution.py:25
  59.4 44.9 %collective-permute-start.23 = (f32[128,1024]{1,0:T(8,128)S(1)}, f32[128,1024]{1,0:T(8,128)S(1)}, u32[]{:S(2)}, u32[]{:S(2)}) collective-permute-start(f32[128,1024]{1,0:T(8,128)S(1)} %collective-permute-done.22), channel_id=1, source_target_pairs={{0,2},{2,4},{4,6},{6,8},{8,10},{10,12},{12,14},{14,0},{1,3},{3,5},... | collective-permute-start | bytes 1572872 | tf_op jit(solution)/shard_map/ppermute | solution.py:25
  59.4 44.9 %collective-permute-start.4 = (f32[128,1024]{1,0:T(8,128)S(1)}, f32[128,1024]{1,0:T(8,128)S(1)}, u32[]{:S(2)}, u32[]{:S(2)}) collective-permute-start(f32[128,1024]{1,0:T(8,128)S(1)} %get-tuple-element.9), channel_id=1, source_target_pairs={{2,0},{4,2},{6,4},{8,6},{10,8},{12,10},{14,12},{0,14},{3,1},{5,3},... | collective-permute-start | bytes 1572872 | tf_op jit(solution)/shard_map/ppermute | solution.py:28
  62.6 46.0 %collective-permute-start.26 = (f32[128,1024]{1,0:T(8,128)S(1)}, f32[128,1024]{1,0:T(8,128)S(1)}, u32[]{:S(2)}, u32[]{:S(2)}) collective-permute-start(f32[128,1024]{1,0:T(8,128)S(1)} %get-tuple-element.10), channel_id=1, source_target_pairs={{2,0},{4,2},{6,4},{8,6},{10,8},{12,10},{14,12},{0,14},{3,1},{5,3},... | collective-permute-start | bytes 1572872 | tf_op jit(solution)/shard_map/ppermute | solution.py:28
  81.8 45.0 %collective-permute-start.1 = (f32[128,1024]{1,0:T(8,128)S(1)}, f32[128,1024]{1,0:T(8,128)}, u32[]{:S(2)}, u32[]{:S(2)}) collective-permute-start(f32[128,1024]{1,0:T(8,128)S(1)} %collective-permute-done), channel_id=1, source_target_pairs={{0,2},{2,4},{4,6},{6,8},{8,10},{10,12},{12,14},{14,0},{1,3},{3,5},... | collective-permute-start | bytes 1572872 | tf_op jit(solution)/shard_map/ppermute | solution.py:25
  104.3 45.0 %collective-permute-start.24 = (f32[128,1024]{1,0:T(8,128)S(1)}, f32[128,1024]{1,0:T(8,128)}, u32[]{:S(2)}, u32[]{:S(2)}) collective-permute-start(f32[128,1024]{1,0:T(8,128)S(1)} %collective-permute-done.23), channel_id=1, source_target_pairs={{0,2},{2,4},{4,6},{6,8},{8,10},{10,12},{12,14},{14,0},{1,3},{3,5},... | collective-permute-start | bytes 1572872 | tf_op jit(solution)/shard_map/ppermute | solution.py:25
  104.3 47.7 %collective-permute-start.5 = (f32[128,1024]{1,0:T(8,128)S(1)}, f32[128,1024]{1,0:T(8,128)}, u32[]{:S(2)}, u32[]{:S(2)}) collective-permute-start(f32[128,1024]{1,0:T(8,128)S(1)} %collective-permute-done.4), channel_id=1, source_target_pairs={{2,0},{4,2},{6,4},{8,6},{10,8},{12,10},{14,12},{0,14},{3,1},{5,3},... | collective-permute-start | bytes 1572872 | tf_op jit(solution)/shard_map/ppermute | solution.py:28
  108.6 46.7 %collective-permute-start.27 = (f32[128,1024]{1,0:T(8,128)S(1)}, f32[128,1024]{1,0:T(8,128)}, u32[]{:S(2)}, u32[]{:S(2)}) collective-permute-start(f32[128,1024]{1,0:T(8,128)S(1)} %collective-permute-done.26), channel_id=1, source_target_pairs={{2,0},{4,2},{6,4},{8,6},{10,8},{12,10},{14,12},{0,14},{3,1},{5,3},... | collective-permute-start | bytes 1572872 | tf_op jit(solution)/shard_map/ppermute | solution.py:28
  126.9 44.9 %collective-permute-start.2 = (f32[128,1024]{1,0:T(8,128)}, f32[128,1024]{1,0:T(8,128)}, u32[]{:S(2)}, u32[]{:S(2)}) collective-permute-start(f32[128,1024]{1,0:T(8,128)} %collective-permute-done.1), channel_id=1, source_target_pairs={{0,2},{2,4},{4,6},{6,8},{8,10},{10,12},{12,14},{14,0},{1,3},{3,5},... | collective-permute-start | bytes 1572872 | tf_op jit(solution)/shard_map/ppermute | solution.py:25
  149.3 44.9 %collective-permute-start.25 = (f32[128,1024]{1,0:T(8,128)}, f32[128,1024]{1,0:T(8,128)}, u32[]{:S(2)}, u32[]{:S(2)}) collective-permute-start(f32[128,1024]{1,0:T(8,128)} %collective-permute-done.24), channel_id=1, source_target_pairs={{0,2},{2,4},{4,6},{6,8},{8,10},{10,12},{12,14},{14,0},{1,3},{3,5},... | collective-permute-start | bytes 1572872 | tf_op jit(solution)/shard_map/ppermute | solution.py:25
  152.0 72.5 %collective-permute-start.6 = (f32[128,1024]{1,0:T(8,128)}, f32[128,1024]{1,0:T(8,128)S(1)}, u32[]{:S(2)}, u32[]{:S(2)}) collective-permute-start(f32[128,1024]{1,0:T(8,128)} %collective-permute-done.5), channel_id=1, source_target_pairs={{2,0},{4,2},{6,4},{8,6},{10,8},{12,10},{14,12},{0,14},{3,1},{5,3},... | collective-permute-start | bytes 1572872 | tf_op jit(solution)/shard_map/ppermute | solution.py:28
  155.2 78.4 %collective-permute-start.28 = (f32[128,1024]{1,0:T(8,128)}, f32[128,1024]{1,0:T(8,128)}, u32[]{:S(2)}, u32[]{:S(2)}) collective-permute-start(f32[128,1024]{1,0:T(8,128)} %collective-permute-done.27), channel_id=1, source_target_pairs={{2,0},{4,2},{6,4},{8,6},{10,8},{12,10},{14,12},{0,14},{3,1},{5,3},... | collective-permute-start | bytes 1572872 | tf_op jit(solution)/shard_map/ppermute | solution.py:28
  171.8 43.3 %collective-permute-start.3 = (f32[128,1024]{1,0:T(8,128)}, f32[128,1024]{1,0:T(8,128)S(1)}, u32[]{:S(2)}, u32[]{:S(2)}) collective-permute-start(f32[128,1024]{1,0:T(8,128)} %collective-permute-done.2), channel_id=1, source_target_pairs={{0,2},{2,4},{4,6},{6,8},{8,10},{10,12},{12,14},{14,0},{1,3},{3,5},... | collective-permute-start | bytes 1572872 | tf_op jit(solution)/shard_map/ppermute | solution.py:25
  337.1 22.5 %collective-permute-start.8 = (f32[128,1024]{1,0:T(8,128)S(1)}, f32[128,1024]{1,0:T(8,128)S(1)}, u32[]{:S(2)}, u32[]{:S(2)}) collective-permute-start(f32[128,1024]{1,0:T(8,128)S(1)} %collective-permute-done.7), channel_id=1, source_target_pairs={{0,2},{2,4},{4,6},{6,8},{8,10},{10,12},{12,14},{14,0},{1,3},{3,5},... | collective-permute-start | bytes 1572872 | tf_op jit(solution)/shard_map/ppermute | solution.py:25
  337.1 23.8 %collective-permute-start.11 = (f32[128,1024]{1,0:T(8,128)S(1)}, f32[128,1024]{1,0:T(8,128)S(1)}, u32[]{:S(2)}, u32[]{:S(2)}) collective-permute-start(f32[128,1024]{1,0:T(8,128)S(1)} %fusion.35), channel_id=1, source_target_pairs={{2,0},{4,2},{6,4},{8,6},{10,8},{12,10},{14,12},{0,14},{3,1},{5,3},... | collective-permute-start | bytes 1572872 | tf_op jit(solution)/shard_map/ppermute | solution.py:28
  340.4 23.9 %collective-permute-start.33 = (f32[128,1024]{1,0:T(8,128)S(1)}, f32[128,1024]{1,0:T(8,128)S(1)}, u32[]{:S(2)}, u32[]{:S(2)}) collective-permute-start(f32[128,1024]{1,0:T(8,128)S(1)} %fusion.31), channel_id=1, source_target_pairs={{2,0},{4,2},{6,4},{8,6},{10,8},{12,10},{14,12},{0,14},{3,1},{5,3},... | collective-permute-start | bytes 1572872 | tf_op jit(solution)/shard_map/ppermute | solution.py:28
  360.9 27.6 %collective-permute-start.12 = (f32[128,1024]{1,0:T(8,128)S(1)}, f32[128,1024]{1,0:T(8,128)S(1)}, u32[]{:S(2)}, u32[]{:S(2)}) collective-permute-start(f32[128,1024]{1,0:T(8,128)S(1)} %collective-permute-done.11), channel_id=1, source_target_pairs={{2,0},{4,2},{6,4},{8,6},{10,8},{12,10},{14,12},{0,14},{3,1},{5,3},... | collective-permute-start | bytes 1572872 | tf_op jit(solution)/shard_map/ppermute | solution.py:28
  364.2 27.6 %collective-permute-start.34 = (f32[128,1024]{1,0:T(8,128)S(1)}, f32[128,1024]{1,0:T(8,128)}, u32[]{:S(2)}, u32[]{:S(2)}) collective-permute-start(f32[128,1024]{1,0:T(8,128)S(1)} %collective-permute-done.33), channel_id=1, source_target_pairs={{2,0},{4,2},{6,4},{8,6},{10,8},{12,10},{14,12},{0,14},{3,1},{5,3},... | collective-permute-start | bytes 1572872 | tf_op jit(solution)/shard_map/ppermute | solution.py:28
  370.8 22.6 %collective-permute-start.31 = (f32[128,1024]{1,0:T(8,128)S(1)}, f32[128,1024]{1,0:T(8,128)}, u32[]{:S(2)}, u32[]{:S(2)}) collective-permute-start(f32[128,1024]{1,0:T(8,128)S(1)} %collective-permute-done.30), channel_id=1, source_target_pairs={{0,2},{2,4},{4,6},{6,8},{8,10},{10,12},{12,14},{14,0},{1,3},{3,5},... | collective-permute-start | bytes 1572872 | tf_op jit(solution)/shard_map/ppermute | solution.py:25
  391.9 38.2 %collective-permute-start.35 = (f32[128,1024]{1,0:T(8,128)}, f32[128,1024]{1,0:T(8,128)}, u32[]{:S(2)}, u32[]{:S(2)}) collective-permute-start(f32[128,1024]{1,0:T(8,128)} %collective-permute-done.34), channel_id=1, source_target_pairs={{2,0},{4,2},{6,4},{8,6},{10,8},{12,10},{14,12},{0,14},{3,1},{5,3},... | collective-permute-start | bytes 1572872 | tf_op jit(solution)/shard_map/ppermute | solution.py:28
  393.4 27.7 %collective-permute-start.32 = (f32[128,1024]{1,0:T(8,128)}, f32[128,1024]{1,0:T(8,128)}, u32[]{:S(2)}, u32[]{:S(2)}) collective-permute-start(f32[128,1024]{1,0:T(8,128)} %collective-permute-done.31), channel_id=1, source_target_pairs={{0,2},{2,4},{4,6},{6,8},{8,10},{10,12},{12,14},{14,0},{1,3},{3,5},... | collective-permute-start | bytes 1572872 | tf_op jit(solution)/shard_map/ppermute | solution.py:25
  421.0 22.6 %collective-permute-start.14 = (f32[128,1024]{1,0:T(8,128)S(1)}, f32[128,1024]{1,0:T(8,128)S(1)}, u32[]{:S(2)}, u32[]{:S(2)}) collective-permute-start(f32[128,1024]{1,0:T(8,128)S(1)} %fusion.34), channel_id=1, source_target_pairs={{0,2},{2,4},{4,6},{6,8},{8,10},{10,12},{12,14},{14,0},{1,3},{3,5},... | collective-permute-start | bytes 1572872 | tf_op jit(solution)/shard_map/ppermute | solution.py:25
  443.6 25.4 %collective-permute-start.15 = (f32[128,1024]{1,0:T(8,128)S(1)}, f32[128,1024]{1,0:T(8,128)S(1)}, u32[]{:S(2)}, u32[]{:S(2)}) collective-permute-start(f32[128,1024]{1,0:T(8,128)S(1)} %collective-permute-done.14), channel_id=1, source_target_pairs={{0,2},{2,4},{4,6},{6,8},{8,10},{10,12},{12,14},{14,0},{1,3},{3,5},... | collective-permute-start | bytes 1572872 | tf_op jit(solution)/shard_map/ppermute | solution.py:25
  444.6 26.4 %collective-permute-start.18 = (f32[128,1024]{1,0:T(8,128)S(1)}, f32[128,1024]{1,0:T(8,128)S(1)}, u32[]{:S(2)}, u32[]{:S(2)}) collective-permute-start(f32[128,1024]{1,0:T(8,128)S(1)} %fusion.34), channel_id=1, source_target_pairs={{2,0},{4,2},{6,4},{8,6},{10,8},{12,10},{14,12},{0,14},{3,1},{5,3},... | collective-permute-start | bytes 1572872 | tf_op jit(solution)/shard_map/ppermute | solution.py:28
  446.9 26.8 %collective-permute-start.40 = (f32[128,1024]{1,0:T(8,128)S(1)}, f32[128,1024]{1,0:T(8,128)S(1)}, u32[]{:S(2)}, u32[]{:S(2)}) collective-permute-start(f32[128,1024]{1,0:T(8,128)S(1)} %fusion.30), channel_id=1, source_target_pairs={{2,0},{4,2},{6,4},{8,6},{10,8},{12,10},{14,12},{0,14},{3,1},{5,3},... | collective-permute-start | bytes 1572872 | tf_op jit(solution)/shard_map/ppermute | solution.py:28
  471.0 29.2 %collective-permute-start.19 = (f32[128,1024]{1,0:T(8,128)S(1)}, f32[128,1024]{1,0:T(8,128)S(1)}, u32[]{:S(2)}, u32[]{:S(2)}) collective-permute-start(f32[128,1024]{1,0:T(8,128)S(1)} %collective-permute-done.18), channel_id=1, source_target_pairs={{2,0},{4,2},{6,4},{8,6},{10,8},{12,10},{14,12},{0,14},{3,1},{5,3},... | collective-permute-start | bytes 1572872 | tf_op jit(solution)/shard_map/ppermute | solution.py:28
  473.7 29.2 %collective-permute-start.41 = (f32[128,1024]{1,0:T(8,128)S(1)}, f32[128,1024]{1,0:T(8,128)}, u32[]{:S(2)}, u32[]{:S(2)}) collective-permute-start(f32[128,1024]{1,0:T(8,128)S(1)} %collective-permute-done.40), channel_id=1, source_target_pairs={{2,0},{4,2},{6,4},{8,6},{10,8},{12,10},{14,12},{0,14},{3,1},{5,3},... | collective-permute-start | bytes 1572872 | tf_op jit(solution)/shard_map/ppermute | solution.py:28
  480.3 23.4 %collective-permute-start.38 = (f32[128,1024]{1,0:T(8,128)S(1)}, f32[128,1024]{1,0:T(8,128)S(1)}, u32[]{:S(2)}, u32[]{:S(2)}) collective-permute-start(f32[128,1024]{1,0:T(8,128)S(1)} %collective-permute-done.37), channel_id=1, source_target_pairs={{0,2},{2,4},{4,6},{6,8},{8,10},{10,12},{12,14},{14,0},{1,3},{3,5},... | collective-permute-start | bytes 1572872 | tf_op jit(solution)/shard_map/ppermute | solution.py:25
  500.2 27.7 %collective-permute-start.20 = (f32[128,1024]{1,0:T(8,128)S(1)}, f32[128,1024]{1,0:T(8,128)S(1)}, u32[]{:S(2)}, u32[]{:S(2)}) collective-permute-start(f32[128,1024]{1,0:T(8,128)S(1)} %collective-permute-done.19), channel_id=1, source_target_pairs={{2,0},{4,2},{6,4},{8,6},{10,8},{12,10},{14,12},{0,14},{3,1},{5,3},... | collective-permute-start | bytes 1572872 | tf_op jit(solution)/shard_map/ppermute | solution.py:28
  502.8 33.7 %collective-permute-start.42 = (f32[128,1024]{1,0:T(8,128)}, f32[128,1024]{1,0:T(8,128)}, u32[]{:S(2)}, u32[]{:S(2)}) collective-permute-start(f32[128,1024]{1,0:T(8,128)} %collective-permute-done.41), channel_id=1, source_target_pairs={{2,0},{4,2},{6,4},{8,6},{10,8},{12,10},{14,12},{0,14},{3,1},{5,3},... | collective-permute-start | bytes 1572872 | tf_op jit(solution)/shard_map/ppermute | solution.py:28
  (30 other events, 759.4 us)
Sparse Core Ops, SparseCore 0:
  38.1 270.6 all-reduce.2
